TPU v7x, 32 devices: a whole 2x2x4 slice. The times are simulated.
32 devices in a mesh: group: 4 (over y, core), freq: 8 (over z, x).
Axes of the slice: x: 2, y: 2, z: 4, core: 2. Of those that a mesh axis runs over, the one named last changes fastest.
Arguments:
- spectra: bfloat16 [2048, 2, 16], P('freq', None, 'group'), may hold values from -6 to 6
- templates: bfloat16 [2048, 2, 2560], P('freq', None, 'group'), may hold values from -600 to 600
- valid_start: int32 [16], replicated, may hold values from 0 to 2048
Outputs:
- peaks: float32 [2560, 16], P('group')
All inputs are finite; a program needn't handle non-finite values.
Results may differ from a plain program's by a relative error of at most 0.0019.
Values may be sent and summed in bfloat16 or wider, within the bound.
A program may use at most 256 MiB of HBM per device.

v0:
```python
import math
import jax
import jax.numpy as jnp
from jax import lax
from jax.sharding import PartitionSpec as P

N = 4096
VALID = 2048


def make_table(bins_count, lag_index):
    bins_index = jnp.arange(bins_count, dtype=jnp.int32)
    angle = (bins_index[:, None] * lag_index[None, :] % N).astype(jnp.float32) * (2.0 * math.pi / N)
    cosine = jnp.cos(angle)
    sine_part = jnp.sin(angle)
    upper = jnp.concatenate([cosine, sine_part], 1)
    lower = jnp.concatenate([-sine_part, cosine], 1)
    return jnp.concatenate([upper, lower], 0).astype(jnp.bfloat16)


def make_cross(bank_piece, seg_piece):
    bank_re = bank_piece[:, 0, :].astype(jnp.float32)[:, None, :]
    bank_im = bank_piece[:, 1, :].astype(jnp.float32)[:, None, :]
    seg_re = seg_piece[:, 0, :].astype(jnp.float32)[:, :, None]
    seg_im = seg_piece[:, 1, :].astype(jnp.float32)[:, :, None]
    cross_re = bank_re * seg_re + bank_im * seg_im
    cross_im = bank_re * seg_im - bank_im * seg_re
    joined = jnp.stack([cross_re, cross_im], 0).astype(jnp.bfloat16)
    return joined.reshape(2 * joined.shape[1], joined.shape[2] * joined.shape[3])


def contract(cross, table):
    return lax.dot_general(
        cross, table, (((0,), (0,)), ((), ())), preferred_element_type=jnp.float32
    )


def on_device(spectra, templates, valid_start):
    freq_count = lax.axis_size("freq")
    lag_count = N // freq_count
    lag_index = lax.axis_index("freq") * lag_count + jnp.arange(lag_count, dtype=jnp.int32)
    tpl_rows = templates.shape[2]
    every_segment = lax.all_gather(spectra, "group", axis=2, tiled=True)
    count = every_segment.shape[2]
    bank_piece = lax.all_gather(templates, "freq", axis=0, tiled=True)
    seg_piece = lax.all_gather(every_segment, "freq", axis=0, tiled=True)
    width = bank_piece.shape[0]
    cross = make_cross(bank_piece, seg_piece)
    series = contract(cross, make_table(width, lag_index))
    bank_float = bank_piece.astype(jnp.float32)
    norm_sum = jnp.sum(bank_float * bank_float, axis=(0, 1))
    series, template_norm = (series, norm_sum)
    power = (
        series[:, :lag_count] * series[:, :lag_count]
        + series[:, lag_count:] * series[:, lag_count:]
    )
    power = power.reshape(count, tpl_rows, lag_count) / template_norm[None, :, None]
    inside = (lag_index[None, :] >= valid_start[:, None]) & (
        lag_index[None, :] < valid_start[:, None] + VALID
    )
    peaks = jnp.max(jnp.where(inside[:, None, :], power, jnp.float32(0.0)), axis=2).T
    return lax.pmax(peaks, "freq")


def solution(mesh):
    in_specs = (P("freq", None, "group"), P("freq", None, "group"), P())
    out_specs = P("group", None)
    return jax.shard_map(
        on_device, mesh=mesh, in_specs=in_specs, out_specs=out_specs, check_vma=False
    )
```

profile of v0, /device:TPU:0, one launch (start us, length us, event | category | flops | bytes accessed | tf_op | source)
XLA Modules:
  0.0 411.2 jit_solution(10462110616772859024)
XLA Ops:
  6.5 2.0 copy.14
  8.5 0.0 all-gather.2.cloned.1.call-update
  8.6 0.7 copy.15
  9.3 6.3 %all_gather.10 = bf16[256,2,16]{0,1,2:T(2,128)(2,1)S(1)} all-gather(bf16[256,2,4]{0,1,2:T(2,128)(2,1)S(1)} %copy.15), channel_id=1, replica_groups=mesh['group'=4,'freq'=8] {'group'}, dimensions={2}, use_global_device_ids=true | all-gather | bytes 20480 | tf_op jit(solution)/shard_map/all_gather | solution.py:43
  15.5 23.8 %all_gather.11 = bf16[2048,2,16]{0,1,2:T(2,128)(2,1)S(1)} all-gather(bf16[256,2,16]{0,1,2:T(2,128)(2,1)S(1)} %all_gather.10), channel_id=1, replica_groups=mesh['group'=4,'freq'=8] {'freq'}, dimensions={0}, use_global_device_ids=true | all-gather | bytes 147456 | tf_op jit(solution)/shard_map/all_gather | solution.py:46
  39.3 0.2 slice_convert_fusion.1
  39.5 0.3 copy.18
  39.9 0.3 copy.19
  40.2 0.7 broadcast_add_fusion
  40.9 0.7 compare_and_fusion
  41.6 0.2 copy.13
  41.8 2.8 broadcast_in_dim.10
  44.6 5.5 %copy.20 = pred[64,8,16,640]{3,1,2,0:T(8,128)(4,1)} copy(pred[64,8,16,640]{3,2,1,0:T(8,128)(4,1)S(1)} %bitcast.22) | data formatting | bytes 10485760
  50.2 18.7 %fusion.21 = (bf16[2048,512]{1,0:T(8,128)(2,1)}, bf16[2048,512]{1,0:T(8,128)(2,1)}, bf16[2048,512]{1,0:T(8,128)(2,1)}) fusion(s32[512]{0:T(512)S(1)} %iota_add_fusion), kind=kLoop, calls=%fused_computation.34 | loop fusion | flops 18874368 | bytes 6293504 | tf_op jit(solution)/shard_map/convert.9
  68.8 30.4 %all-gather.2.cloned.1.call-done = bf16[2048,2,640]{2,0,1:T(8,128)(2,1)} async-done(((bf16[256,2,640]{2,0,1:T(8,128)(2,1)}), bf16[2048,2,640]{2,0,1:T(8,128)(2,1)}) %all-gather.2.cloned.1.call-update) | async-done | bytes 5242896 | tf_op jit(solution)/shard_map/all_gather | solution.py:45
  99.2 7.2 %fusion.19 = (f32[2048,640]{1,0:T(8,128)}, f32[2048,640]{1,0:T(8,128)}) fusion(bf16[2048,2,640]{2,0,1:T(8,128)(2,1)} %all-gather.2.cloned.1.call-done), kind=kLoop, calls=%fused_computation.32 | loop fusion | flops 2621440 | bytes 15728640 | tf_op jit(solution)/shard_map/mul | solution.py:26
  106.4 31.5 %add_convert_fusion = (bf16[1,2048,16,640]{3,2,1,0:T(8,128)(2,1)}, bf16[1,2048,16,640]{3,2,1,0:T(8,128)(2,1)}) fusion(f32[2048,16]{1,0:T(8,128)S(1)} %bitcast.25, f32[2048,640]{1,0:T(8,128)} %get-tuple-element.8, f32[2048,16]{1,0:T(8,128)S(1)} %bitcast.24, f32[2048,640]{1,0:T(8,128)} %get-tuple-element.7), kind=kLoop, calls=%fused_computation.2 | loop fusion | flops 167772160 | bytes 94633984 | tf_op jit(solution)/shard_map/convert.10
  137.9 56.2 %pad_maximum_fusion = bf16[2,2048,16,640]{3,2,1,0:T(8,128)(2,1)} fusion(bf16[1,2048,16,640]{3,2,1,0:T(8,128)(2,1)} %get-tuple-element.6, bf16[1,2048,16,640]{3,2,1,0:T(8,128)(2,1)} %get-tuple-element.5), kind=kLoop, calls=%fused_computation | loop fusion | flops 41943040 | bytes 167772160 | tf_op jit(solution)/shard_map/stack | solution.py:28
  194.1 55.4 %copy.21 = bf16[512,8,16,640]{3,1,2,0:T(8,128)(2,1)} copy(bf16[512,8,16,640]{3,2,1,0:T(8,128)(2,1)} %bitcast.12) | data formatting | bytes 167772160
  249.5 3.6 multiply_reduce_fusion
  253.1 0.6 div.14
  253.7 99.3 %fusion.4 = f32[10240,1024]{0,1:T(8,128)} fusion(bf16[4096,10240]{1,0:T(8,128)(2,1)} %bitcast.13, bf16[2048,512]{1,0:T(8,128)(2,1)} %get-tuple-element.13, bf16[2048,512]{1,0:T(8,128)(2,1)} %get-tuple-element.12, bf16[2048,512]{1,0:T(8,128)(2,1)S(1)} %copy-done), kind=kOutput, calls=%fused_computation.10 | convolution fusion | flops 85932900352 | bytes 132120576 | tf_op jit(solution)/shard_map/dot_general | solution.py:33
  353.0 15.9 %fusion.3 = f32[10240]{0:T(1024)S(1)} fusion(pred[10240,512]{0,1:T(8,128)(4,1)} %bitcast.23, f32[10240,1024]{0,1:T(8,128)} %fusion.4, f32[10240]{0:T(1024)S(1)} %copy-done.1), kind=kLoop, calls=%fused_computation.8 | loop fusion | flops 31447040 | bytes 47267840 | tf_op jit(solution)/shard_map/reduce_max | solution.py:61
  369.0 35.3 %pmax.7 = f32[640,16]{0,1:T(8,128)} all-reduce(f32[640,16]{0,1:T(8,128)S(1)} %bitcast.26), channel_id=1, replica_groups=mesh['group'=4,'freq'=8] {'freq'}, use_global_device_ids=true, to_apply=%region_2.3 | all-reduce | flops 10240 | bytes 81920 | tf_op jit(solution)/shard_map/pmax | solution.py:62
  (8 shorter events, 0.0 us)
Async XLA Ops:
  6.5 92.7 %all-gather.2.cloned.1.call-start = ((), (), s32[]{:S(2)}) async-start(), calls=%async_computation | async-start | bytes 5898240 | tf_op jit(solution)/shard_map/all_gather | solution.py:45
  194.1 59.7 %copy-start = (bf16[2048,512]{1,0:T(8,128)(2,1)S(1)}, bf16[2048,512]{1,0:T(8,128)(2,1)}, u32[]{:S(2)}) copy-start(bf16[2048,512]{1,0:T(8,128)(2,1)} %get-tuple-element.11) | copy-start | bytes 6291460
  253.7 99.3 %copy-start.1 = (f32[10240]{0:T(1024)S(1)}, f32[10240]{0:T(1024)}, u32[]{:S(2)}) copy-start(f32[10240]{0:T(1024)} %div.14) | copy-start | bytes 122884
Sparse Core Ops, SparseCore 0:
  9.5 89.6 all-gather.1
where the time goes:
time: 411 us
  other arithmetic  135 us (33%)
  matrix products  99.3 us (24%)
  local copies, waits for them, and re-layouts  68 us (17%)
  blocking collectives  65.4 us (16%)
  waiting for transfers between devices  30.4 us (7%)
  between operations  13.5 us (3%)
    dot_general x1, matrix products, contract(): lax.dot_general(cross, table, (((0,), (0,)), ((), ())), preferred_element...  99.3 us
    unnamed x8, local copies, waits for them, and re-layouts  63.7 us
    another operation x1, other arithmetic, make_cross(): joined = jnp.stack([cross_re, cross_im], 0).astype(jnp.bfloat16)  56.2 us
    another operation x2, other arithmetic  50.2 us
    pmax x1, blocking collectives, on_device(): return lax.pmax(peaks, 'freq')  35.3 us
    all_gather x1, waiting for transfers between devices, on_device(): bank_piece = lax.all_gather(templates, 'freq', axis=0, tiled=True)  30.4 us
    all_gather x1, blocking collectives, on_device(): seg_piece = lax.all_gather(every_segment, 'freq', axis=0, tiled=True)  23.8 us
    reduce_max x1, other arithmetic, on_device(): jnp.max(jnp.where(inside[:, None, :], power, jnp.float32(0.0)), axis=2)  15.9 us
  transfers between devices with their start and end apart: 1, of which 1 were waited for; matrix products, arithmetic and copies ran while one was open for 7% of the time, Pallas kernels for 0%

commit v1 on v0

--- a/solution.py
+++ b/solution.py
@@ -42,7 +42,9 @@
     tpl_rows = templates.shape[2]
     every_segment = lax.all_gather(spectra, "group", axis=2, tiled=True)
     count = every_segment.shape[2]
-    bank_piece = lax.all_gather(templates, "freq", axis=0, tiled=True)
+    bank_piece = jnp.concatenate(
+        lax.all_to_all(jnp.stack([templates] * lax.axis_size("freq")), "freq", 0, 0), axis=0
+    )
     seg_piece = lax.all_gather(every_segment, "freq", axis=0, tiled=True)
     width = bank_piece.shape[0]
     cross = make_cross(bank_piece, seg_piece)

time: 411 us -> 471 us (1.15)
  blocking collectives: 65.4 us -> 161 us
  waiting for transfers between devices: 30.4 us -> 0.01 us
  between operations: 13.5 us -> 0.13 us
  starting transfers between devices: 0.01 us -> 7.28 us
    all_gather x1, blocking collectives: 23.8 us -> 114 us  [on_device(): seg_piece = lax.all_gather(every_segment, 'freq', axis=0, tiled=True)]
    all_gather x1 -> x0, waiting for transfers between devices: 30.4 us -> none  [on_device(): bank_piece = lax.all_gather(templates, 'freq', axis=0, tiled=True)]
    all_to_all x0 -> x1, starting transfers between devices: none -> 7.28 us  [on_device(): lax.all_to_all(jnp.stack([templates] * lax.axis_size('freq')), 'freq', 0, 0)]
    pmax x1, blocking collectives: 35.3 us -> 41.8 us  [on_device(): return lax.pmax(peaks, 'freq')]
    unnamed x8 -> x12, local copies, waits for them, and re-layouts: 63.7 us -> 62.1 us
  transfers between devices with their start and end apart: 1 -> 1, of which waited for: 1 -> 0; matrix products, arithmetic and copies ran while one was open for 7% -> 6% of each run, Pallas kernels for 0% -> 0%
where the time goes in v1:
time: 471 us
  blocking collectives  161 us (34%)
  other arithmetic  131 us (28%)
  matrix products  99.3 us (21%)
  local copies, waits for them, and re-layouts  72.3 us (15%)
  starting transfers between devices  7.28 us (2%)
    all_gather x1, blocking collectives, on_device(): seg_piece = lax.all_gather(every_segment, 'freq', axis=0, tiled=True)  114 us
    dot_general x1, matrix products, contract(): lax.dot_general(cross, table, (((0,), (0,)), ((), ())), preferred_element...  99.3 us
    unnamed x12, local copies, waits for them, and re-layouts  62.1 us
    another operation x1, other arithmetic, make_cross(): joined = jnp.stack([cross_re, cross_im], 0).astype(jnp.bfloat16)  56.2 us
    another operation x2, other arithmetic  50.2 us
    pmax x1, blocking collectives, on_device(): return lax.pmax(peaks, 'freq')  41.8 us
    reduce_max x1, other arithmetic, on_device(): jnp.max(jnp.where(inside[:, None, :], power, jnp.float32(0.0)), axis=2)  15.9 us
  transfers between devices with their start and end apart: 1, of which 0 were waited for; matrix products, arithmetic and copies ran while one was open for 6% of the time, Pallas kernels for 0%

profile of v1, /device:TPU:0, one launch (start us, length us, event | category | flops | bytes accessed | tf_op | source)
XLA Modules:
  0.0 470.8 jit_solution(11588537818297493)
XLA Ops:
  0.0 1.2 copy.15
  1.2 0.0 copy-start.3
  1.2 2.9 stack.5
  4.1 7.3 %all-to-all-start = ((bf16[8,256,2,640]{3,1,2,0:T(8,128)(2,1)}), bf16[8,256,2,640]{3,1,2,0:T(8,128)(2,1)}, u32[]{:S(2)}, u32[]{:S(2)}) async-start(bf16[8,256,2,640]{3,1,2,0:T(8,128)(2,1)} %stack.5), calls=%async_computation | async-start | bytes 10485760 | tf_op jit(solution)/shard_map/all_to_all | solution.py:46
  11.4 5.2 %all_gather.6 = bf16[256,2,16]{0,1,2:T(2,128)(2,1)S(1)} all-gather(bf16[256,2,4]{0,1,2:T(2,128)(2,1)S(1)} %copy.17), channel_id=1, replica_groups=mesh['group'=4,'freq'=8] {'group'}, dimensions={2}, use_global_device_ids=true | all-gather | bytes 20480 | tf_op jit(solution)/shard_map/all_gather | solution.py:43
  16.6 114.0 %all_gather.7 = bf16[2048,2,16]{0,1,2:T(2,128)(2,1)S(1)} all-gather(bf16[256,2,16]{0,1,2:T(2,128)(2,1)S(1)} %all_gather.6), channel_id=1, replica_groups=mesh['group'=4,'freq'=8] {'freq'}, dimensions={0}, use_global_device_ids=true | all-gather | bytes 147456 | tf_op jit(solution)/shard_map/all_gather | solution.py:48
  130.6 0.2 slice_convert_fusion.1
  130.8 0.3 copy.20
  131.2 0.3 copy.21
  131.5 0.1 compare_and_fusion
  131.6 0.2 copy.14
  131.8 2.8 broadcast_in_dim.10
  134.7 5.5 %copy.22 = pred[64,8,16,640]{3,1,2,0:T(8,128)(4,1)} copy(pred[64,8,16,640]{3,2,1,0:T(8,128)(4,1)S(1)} %bitcast.23) | data formatting | bytes 10485760
  140.2 18.7 %fusion.21 = (bf16[2048,512]{1,0:T(8,128)(2,1)}, bf16[2048,512]{1,0:T(8,128)(2,1)}, bf16[2048,512]{1,0:T(8,128)(2,1)}) fusion(s32[512]{0:T(512)S(1)} %iota_add_fusion), kind=kLoop, calls=%fused_computation.34 | loop fusion | flops 18874368 | bytes 6293504 | tf_op jit(solution)/shard_map/convert.9
  158.8 2.9 copy.16
  161.8 4.6 fusion.19
  166.4 31.5 %add_convert_fusion = (bf16[1,2048,16,640]{3,2,1,0:T(8,128)(2,1)}, bf16[1,2048,16,640]{3,2,1,0:T(8,128)(2,1)}) fusion(f32[2048,16]{1,0:T(8,128)S(1)} %bitcast.27, f32[2048,640]{1,0:T(8,128)} %get-tuple-element.8, f32[2048,16]{1,0:T(8,128)S(1)} %bitcast.26, f32[2048,640]{1,0:T(8,128)} %get-tuple-element.7), kind=kLoop, calls=%fused_computation.2 | loop fusion | flops 167772160 | bytes 94633984 | tf_op jit(solution)/shard_map/convert.10
  197.9 56.2 %pad_maximum_fusion = bf16[2,2048,16,640]{3,2,1,0:T(8,128)(2,1)} fusion(bf16[1,2048,16,640]{3,2,1,0:T(8,128)(2,1)} %get-tuple-element.6, bf16[1,2048,16,640]{3,2,1,0:T(8,128)(2,1)} %get-tuple-element.5), kind=kLoop, calls=%fused_computation | loop fusion | flops 41943040 | bytes 167772160 | tf_op jit(solution)/shard_map/stack | solution.py:28
  254.1 55.4 %copy.23 = bf16[512,8,16,640]{3,1,2,0:T(8,128)(2,1)} copy(bf16[512,8,16,640]{3,2,1,0:T(8,128)(2,1)} %bitcast.13) | data formatting | bytes 167772160
  309.6 3.6 multiply_reduce_fusion
  313.1 0.6 div.14
  313.8 99.3 %fusion.4 = f32[10240,1024]{0,1:T(8,128)} fusion(bf16[4096,10240]{1,0:T(8,128)(2,1)} %bitcast.14, bf16[2048,512]{1,0:T(8,128)(2,1)} %get-tuple-element.13, bf16[2048,512]{1,0:T(8,128)(2,1)} %get-tuple-element.12, bf16[2048,512]{1,0:T(8,128)(2,1)S(1)} %copy-done), kind=kOutput, calls=%fused_computation.10 | convolution fusion | flops 85932900352 | bytes 132120576 | tf_op jit(solution)/shard_map/dot_general | solution.py:33
  413.0 15.9 %fusion.3 = f32[10240]{0:T(1024)S(1)} fusion(pred[10240,512]{0,1:T(8,128)(4,1)} %bitcast.25, f32[10240,1024]{0,1:T(8,128)} %fusion.4, f32[10240]{0:T(1024)S(1)} %copy-done.1), kind=kLoop, calls=%fused_computation.8 | loop fusion | flops 31447040 | bytes 47267840 | tf_op jit(solution)/shard_map/reduce_max | solution.py:63
  429.0 41.8 %pmax.7 = f32[640,16]{0,1:T(8,128)} all-reduce(f32[640,16]{0,1:T(8,128)S(1)} %bitcast.28), channel_id=1, replica_groups=mesh['group'=4,'freq'=8] {'freq'}, use_global_device_ids=true, to_apply=%region_2.3 | all-reduce | flops 10240 | bytes 81920 | tf_op jit(solution)/shard_map/pmax | solution.py:64
  (13 shorter events, 0.0 us)
Async XLA Ops:
  1.2 10.2 %copy-start.2 = (bf16[256,2,4]{0,2,1:T(4,128)(2,1)S(1)}, bf16[256,2,4]{0,2,1:T(4,128)(2,1)}, u32[]{:S(2)}) copy-start(bf16[256,2,4]{0,2,1:T(4,128)(2,1)} %param.3) | copy-start | bytes 12292
  1.2 130.4 %copy-start.3 = (s32[16]{0:T(128)S(1)}, s32[16]{0:T(128)}, u32[]{:S(2)}) copy-start(s32[16]{0:T(128)} %param.5) | copy-start | bytes 196
  4.1 154.7 %all-to-all-start = ((bf16[8,256,2,640]{3,1,2,0:T(8,128)(2,1)}), bf16[8,256,2,640]{3,1,2,0:T(8,128)(2,1)}, u32[]{:S(2)}, u32[]{:S(2)}) async-start(bf16[8,256,2,640]{3,1,2,0:T(8,128)(2,1)} %stack.5), calls=%async_computation | async-start | bytes 10485760 | tf_op jit(solution)/shard_map/all_to_all | solution.py:46
  254.1 59.6 %copy-start = (bf16[2048,512]{1,0:T(8,128)(2,1)S(1)}, bf16[2048,512]{1,0:T(8,128)(2,1)}, u32[]{:S(2)}) copy-start(bf16[2048,512]{1,0:T(8,128)(2,1)} %get-tuple-element.11) | copy-start | bytes 6291460
  313.8 99.3 %copy-start.1 = (f32[10240]{0:T(1024)S(1)}, f32[10240]{0:T(1024)}, u32[]{:S(2)}) copy-start(f32[10240]{0:T(1024)} %div.14) | copy-start | bytes 122884
